TPU v7x, 32 devices: a whole 2x2x4 slice. The times are simulated.
32 devices in a mesh: row: 2 (over x), col: 16 (over z, y, core).
Axes of the slice: x: 2, y: 2, z: 4, core: 2. Of those that a mesh axis runs over, the one named last changes fastest.
Arguments:
- hessian_old: float32 [2048, 12288], P('row', 'col'), may hold values from -6 to 6
- gate_rows: bfloat16 [512, 2048], P('col', 'row'), may hold values from -9 to 9
- up_rows: bfloat16 [512, 2048], P('col', 'row'), may hold values from -15 to 15
- gate_columns: bfloat16 [512, 12288], P('row', 'col'), may hold values from -9 to 9
- up_columns: bfloat16 [512, 12288], P('row', 'col'), may hold values from -15 to 15
Outputs:
- hessian_new: float32 [2048, 12288], P('row', 'col')
All inputs are finite; a program needn't handle non-finite values.
Results may differ from a plain program's by a relative error of at most 0.00099.
Values may be sent and summed in bfloat16 or wider, within the bound.
A program may use at most 64 MiB of HBM per device.

v0:
```python
import jax
import jax.numpy as jnp
from jax import lax
from jax.sharding import PartitionSpec as P


def silu_product(gate, up):
    return (jax.nn.silu(gate.astype(jnp.float32)) * up.astype(jnp.float32)).astype(jnp.bfloat16)


def body(hessian_old, gate_rows, up_rows, gate_columns, up_columns):
    total_tokens = lax.axis_size("col") * gate_rows.shape[0]
    row_formed = silu_product(gate_rows, up_rows)
    column_formed = silu_product(gate_columns, up_columns)
    column_gathered = lax.all_gather(column_formed, "row", axis=0, tiled=True)
    product = lax.dot_general(
        lax.all_gather(row_formed, "col", axis=0, tiled=True),
        column_gathered,
        (((0,), (0,)), ((), ())),
        preferred_element_type=jnp.float32,
    )
    return 0.5 * hessian_old + product / total_tokens


def solution(mesh):
    in_specs = (P("row", "col"), P("col", "row"), P("col", "row"), P("row", "col"), P("row", "col"))
    out_specs = P("row", "col")
    return jax.shard_map(body, mesh=mesh, in_specs=in_specs, out_specs=out_specs, check_vma=False)
```

profile of v0, /device:TPU:0, one launch (start us, length us, event | category | flops | bytes accessed | tf_op | source)
XLA Modules:
  0.0 61.9 jit_solution(4926446980811626307)
XLA Ops:
  6.5 0.0 all-gather.2.cloned.1.call-start
  6.5 1.5 %fusion.9 = bf16[32,1024]{1,0:T(8,128)(2,1)} fusion(bf16[32,1024]{1,0:T(8,128)(2,1)} %param.7, bf16[32,1024]{1,0:T(8,128)(2,1)} %param.6), kind=kLoop, calls=%fused_computation.14 | loop fusion | flops 262144 | bytes 196608 | tf_op jit(solution)/shard_map/convert_element_type | solution.py:8
  8.1 0.0 all-gather.2.cloned.1.call-update
  8.1 1.4 %fusion.4 = bf16[256,768]{1,0:T(8,128)(2,1)S(1)} fusion(bf16[256,768]{1,0:T(8,128)(2,1)} %param.9, bf16[256,768]{1,0:T(8,128)(2,1)} %param.8), kind=kLoop, calls=%fused_computation.7 | loop fusion | flops 1572864 | bytes 1179648 | tf_op jit(solution)/shard_map/convert_element_type | solution.py:8
  9.5 12.8 %all_gather.7 = bf16[512,768]{1,0:T(8,128)(2,1)S(1)} all-gather(bf16[256,768]{1,0:T(8,128)(2,1)S(1)} %fusion.4), channel_id=1, replica_groups=mesh['row'=2,'col'=16] {'row'}, dimensions={0}, use_global_device_ids=true | all-gather | bytes 1179648 | tf_op jit(solution)/shard_map/all_gather | solution.py:15
  22.2 27.9 %all-gather.2.cloned.1.call-done = bf16[512,1024]{1,0:T(8,128)(2,1)} async-done(((bf16[32,1024]{1,0:T(8,128)(2,1)}), bf16[512,1024]{1,0:T(8,128)(2,1)}) %all-gather.2.cloned.1.call-update) | async-done | bytes 1048592 | tf_op jit(solution)/shard_map/all_gather | solution.py:17
  50.1 4.9 %multiply_add_fusion = f32[1024,768]{1,0:T(8,128)} fusion(f32[1024,768]{1,0:T(8,128)} %param.5, bf16[512,1024]{1,0:T(8,128)(2,1)} %all-gather.2.cloned.1.call-done, bf16[512,768]{1,0:T(8,128)(2,1)S(1)} %all_gather.7), kind=kOutput, calls=%fused_computation | convolution fusion | flops 807665664 | bytes 8126464 | tf_op jit(solution)/shard_map/dot_general | solution.py:16
Async XLA Ops:
  6.5 43.6 %all-gather.2.cloned.1.call-start = ((), (), s32[]{:S(2)}) async-start(), calls=%async_computation | async-start | bytes 1114112 | tf_op jit(solution)/shard_map/all_gather | solution.py:17
Sparse Core Ops, SparseCore 0:
  9.5 40.5 all-gather.1
where the time goes:
time: 62.1 us; the launch traced here: 61.9 us
  waiting for transfers between devices  27.9 us (45%)
  between operations  13.4 us (22%)
  blocking collectives  12.8 us (21%)
  matrix products  4.9 us (8%)
  other arithmetic  2.92 us (5%)
    all_gather x1, waiting for transfers between devices, body(): lax.all_gather(row_formed, 'col', axis=0, tiled=True)  27.9 us
    all_gather x1, blocking collectives, body(): column_gathered = lax.all_gather(column_formed, 'row', axis=0, tiled=True)  12.8 us
    dot_general x1, matrix products, body(): lax.dot_general(lax.all_gather(row_formed, 'col', axis=0, tiled=True), co...  4.9 us
    convert_element_type x2, other arithmetic, silu_product(): (jax.nn.silu(gate.astype(jnp.float32)) * up.astype(jnp.float32)).astype(j...  2.92 us
  transfers between devices with their start and end apart: 1, of which 1 were waited for; matrix products, arithmetic and copies ran while one was open for 2% of the time, Pallas kernels for 0%

commit v1 on v0

--- a/solution.py
+++ b/solution.py
@@ -1,7 +1,41 @@
+import functools
 import jax
 import jax.numpy as jnp
 from jax import lax
 from jax.sharding import PartitionSpec as P
+
+
+def bind_the_units(original, axis_k):
+    original = jnp.moveaxis(original, 0, axis_k)
+    o_now = original.shape
+    return original.reshape(
+        *o_now[:axis_k], o_now[axis_k] * o_now[axis_k + 1], *o_now[axis_k + 2 :]
+    )
+
+
+def post_the_stops_all(x_local, device_axis):
+    b_next = lax.psum(1, axis_name=device_axis)
+    r_now, f_next = (b_next, lax.axis_index(device_axis))
+    moved, all_values = (x_local[None], 1)
+    while all_values < r_now:
+        pool = []
+        for ii in range(r_now):
+            pool.append((ii, ii ^ all_values))
+        local_out = lax.ppermute(moved, axis_name=device_axis, perm=pool)
+        res = f_next & all_values == 0
+        moved = jnp.concatenate(
+            [jnp.where(res, moved, local_out), jnp.where(res, local_out, moved)]
+        )
+        all_values *= 2
+    return moved
+
+
+def see_the_orders(obj, z_in, which_dim):
+    h_now = post_the_stops_all(obj, z_in)
+    return bind_the_units(h_now, which_dim)
+
+
+weights_read = functools.partial(see_the_orders, z_in="col", which_dim=0)
 
 
 def silu_product(gate, up):
@@ -14,7 +48,7 @@
     column_formed = silu_product(gate_columns, up_columns)
     column_gathered = lax.all_gather(column_formed, "row", axis=0, tiled=True)
     product = lax.dot_general(
-        lax.all_gather(row_formed, "col", axis=0, tiled=True),
+        weights_read(row_formed),
         column_gathered,
         (((0,), (0,)), ((), ())),
         preferred_element_type=jnp.float32,

time: 62.1 us -> 45.1 us (0.73)
  between operations: 13.4 us -> 0.07 us
  starting transfers between devices: 0.01 us -> 7.94 us
  waiting for transfers between devices: 27.9 us -> 22.6 us
  blocking collectives: 12.8 us -> 9.98 us
  matrix products: 4.9 us -> 2.74 us
  other arithmetic: 2.92 us -> 1.58 us
    all_gather x1 -> x0, waiting for transfers between devices: 27.9 us -> none  [body(): lax.all_gather(row_formed, 'col', axis=0, tiled=True)]
    ppermute x0 -> x4, waiting for transfers between devices: none -> 22.6 us  [post_the_stops_all(): local_out = lax.ppermute(moved, axis_name=device_axis, perm=pool)]
    ppermute x0 -> x4, starting transfers between devices: none -> 7.94 us  [post_the_stops_all(): local_out = lax.ppermute(moved, axis_name=device_axis, perm=pool)]
    all_gather x1, blocking collectives: 12.8 us -> 9.98 us  [body(): column_gathered = lax.all_gather(column_formed, 'row', axis=0, tiled=True)]
    convert_element_type x2 -> x1, other arithmetic: 2.92 us -> 0.25 us  [silu_product(): (jax.nn.silu(gate.astype(jnp.float32)) * up.astype(jnp.float32)).astype(j...]
    dot_general x1, matrix products: 4.9 us -> 2.74 us  [body(): lax.dot_general(weights_read(row_formed), column_gathered, (((0,), (0,)),...]
    broadcast_in_dim x0 -> x1, other arithmetic: none -> 0.99 us  [post_the_stops_all(): moved, all_values = (x_local[None], 1)]
  transfers between devices with their start and end apart: 1 -> 4, of which waited for: 1 -> 4; matrix products, arithmetic and copies ran while one was open for 2% -> 1% of each run, Pallas kernels for 0% -> 0%
where the time goes in v1:
time: 45.1 us; the launch traced here: 44.9 us
  waiting for transfers between devices  22.6 us (50%)
  blocking collectives  9.98 us (22%)
  starting transfers between devices  7.94 us (18%)
  matrix products  2.74 us (6%)
  other arithmetic  1.58 us (4%)
    ppermute x4, waiting for transfers between devices, post_the_stops_all(): local_out = lax.ppermute(moved, axis_name=device_axis, perm=pool)  22.6 us
    all_gather x1, blocking collectives, body(): column_gathered = lax.all_gather(column_formed, 'row', axis=0, tiled=True)  9.98 us
    ppermute x4, starting transfers between devices, post_the_stops_all(): local_out = lax.ppermute(moved, axis_name=device_axis, perm=pool)  7.94 us
    dot_general x1, matrix products, body(): lax.dot_general(weights_read(row_formed), column_gathered, (((0,), (0,)),...  2.74 us
    broadcast_in_dim x1, other arithmetic, post_the_stops_all(): moved, all_values = (x_local[None], 1)  0.99 us
  transfers between devices with their start and end apart: 4, of which 4 were waited for; matrix products, arithmetic and copies ran while one was open for 1% of the time, Pallas kernels for 0%

profile of v1, /device:TPU:0, one launch (start us, length us, event | category | flops | bytes accessed | tf_op | source)
XLA Modules:
  0.0 44.9 jit_solution(648638336323696976)
XLA Ops:
  0.0 0.0 copy-start.1
  0.0 0.0 copy-start.2
  0.0 1.0 %fusion.10 = bf16[1,32,1024]{2,1,0:T(8,128)(2,1)S(1)} fusion(bf16[32,1024]{1,0:T(8,128)(2,1)} %param.7, bf16[32,1024]{1,0:T(8,128)(2,1)} %param.6), kind=kLoop, calls=%fused_computation.25 | loop fusion | flops 262144 | bytes 196608 | tf_op jit(solution)/shard_map/broadcast_in_dim | solution.py:19
  1.0 0.6 %collective-permute-start = (bf16[1,32,1024]{2,1,0:T(8,128)(2,1)S(1)}, bf16[1,32,1024]{2,1,0:T(8,128)(2,1)S(1)}, u32[]{:S(2)}, u32[]{:S(2)}) collective-permute-start(bf16[1,32,1024]{2,1,0:T(8,128)(2,1)S(1)} %fusion.10), channel_id=1, source_target_pairs={{0,1},{1,0},{2,3},{3,2},{4,5},{5,4},{6,7},{7,6},{8,9},{9,8},{10,11... | collective-permute-start | bytes 196616 | tf_op jit(solution)/shard_map/ppermute | solution.py:24
  1.6 0.9 %collective-permute-done = bf16[1,32,1024]{2,1,0:T(8,128)(2,1)S(1)} collective-permute-done((bf16[1,32,1024]{2,1,0:T(8,128)(2,1)S(1)}, bf16[1,32,1024]{2,1,0:T(8,128)(2,1)S(1)}, u32[]{:S(2)}, u32[]{:S(2)}) %collective-permute-start) | collective-permute-done | bytes 65568 | tf_op jit(solution)/shard_map/ppermute | solution.py:24
  2.5 2.9 %collective-permute-start.1 = (bf16[2,32,1024]{2,1,0:T(8,128)(2,1)S(1)}, bf16[2,32,1024]{2,1,0:T(8,128)(2,1)S(1)}, u32[]{:S(2)}, u32[]{:S(2)}) collective-permute-start(bf16[2,32,1024]{2,1,0:T(8,128)(2,1)S(1)} %pad_maximum_fusion.3), channel_id=1, source_target_pairs={{0,2},{1,3},{2,0},{3,1},{4,6},{5,7},{6,4},{7,5},{8,10},{9,11},{10,... | collective-permute-start | bytes 393224 | tf_op jit(solution)/shard_map/ppermute | solution.py:24
  5.4 3.8 %collective-permute-done.1 = bf16[2,32,1024]{2,1,0:T(8,128)(2,1)S(1)} collective-permute-done((bf16[2,32,1024]{2,1,0:T(8,128)(2,1)S(1)}, bf16[2,32,1024]{2,1,0:T(8,128)(2,1)S(1)}, u32[]{:S(2)}, u32[]{:S(2)}) %collective-permute-start.1) | collective-permute-done | bytes 131104 | tf_op jit(solution)/shard_map/ppermute | solution.py:24
  9.3 1.9 %collective-permute-start.2 = (bf16[4,32,1024]{2,1,0:T(8,128)(2,1)S(1)}, bf16[4,32,1024]{2,1,0:T(8,128)(2,1)S(1)}, u32[]{:S(2)}, u32[]{:S(2)}) collective-permute-start(bf16[4,32,1024]{2,1,0:T(8,128)(2,1)S(1)} %pad_maximum_fusion.2), channel_id=1, source_target_pairs={{0,4},{1,5},{2,6},{3,7},{4,0},{5,1},{6,2},{7,3},{8,12},{9,13},{10,... | collective-permute-start | bytes 786440 | tf_op jit(solution)/shard_map/ppermute | solution.py:24
  11.2 6.0 %collective-permute-done.2 = bf16[4,32,1024]{2,1,0:T(8,128)(2,1)S(1)} collective-permute-done((bf16[4,32,1024]{2,1,0:T(8,128)(2,1)S(1)}, bf16[4,32,1024]{2,1,0:T(8,128)(2,1)S(1)}, u32[]{:S(2)}, u32[]{:S(2)}) %collective-permute-start.2) | collective-permute-done | bytes 262176 | tf_op jit(solution)/shard_map/ppermute | solution.py:24
  17.3 2.6 %collective-permute-start.3 = (bf16[8,32,1024]{2,1,0:T(8,128)(2,1)S(1)}, bf16[8,32,1024]{2,1,0:T(8,128)(2,1)S(1)}, u32[]{:S(2)}, u32[]{:S(2)}) collective-permute-start(bf16[8,32,1024]{2,1,0:T(8,128)(2,1)S(1)} %pad_maximum_fusion.1), channel_id=1, source_target_pairs={{0,8},{1,9},{2,10},{3,11},{4,12},{5,13},{6,14},{7,15},{8,0},{9,1},... | collective-permute-start | bytes 1572872 | tf_op jit(solution)/shard_map/ppermute | solution.py:24
  19.9 0.0 copy-done.1
  19.9 0.0 copy-done.2
  19.9 0.0 copy-start
  19.9 0.3 fusion.4
  20.1 10.0 %all_gather.3 = bf16[512,768]{1,0:T(8,128)(2,1)S(1)} all-gather(bf16[256,768]{1,0:T(8,128)(2,1)S(1)} %fusion.4), channel_id=1, replica_groups=mesh['row'=2,'col'=16] {'row'}, dimensions={0}, use_global_device_ids=true | all-gather | bytes 1179648 | tf_op jit(solution)/shard_map/all_gather | solution.py:49
  30.1 11.9 %collective-permute-done.3 = bf16[8,32,1024]{2,1,0:T(8,128)(2,1)S(1)} collective-permute-done((bf16[8,32,1024]{2,1,0:T(8,128)(2,1)S(1)}, bf16[8,32,1024]{2,1,0:T(8,128)(2,1)S(1)}, u32[]{:S(2)}, u32[]{:S(2)}) %collective-permute-start.3) | collective-permute-done | bytes 524320 | tf_op jit(solution)/shard_map/ppermute | solution.py:24
  42.0 0.1 broadcast_select_fusion.1
  42.1 0.1 pad_maximum_fusion
  42.2 0.0 copy-done
  42.2 2.7 %multiply_add_fusion = f32[1024,768]{1,0:T(8,128)} fusion(f32[1024,768]{1,0:T(8,128)S(1)} %copy-done, bf16[512,1024]{1,0:T(8,128)(2,1)S(1)} %bitcast.5, bf16[512,768]{1,0:T(8,128)(2,1)S(1)} %all_gather.3), kind=kOutput, calls=%fused_computation | convolution fusion | flops 807665664 | bytes 8126464 | tf_op jit(solution)/shard_map/dot_general | solution.py:50
  (6 shorter events, 0.2 us)
Async XLA Ops:
  0.0 19.9 %copy-start.1 = (bf16[256,768]{1,0:T(8,128)(2,1)S(1)}, bf16[256,768]{1,0:T(8,128)(2,1)}, u32[]{:S(2)}) copy-start(bf16[256,768]{1,0:T(8,128)(2,1)} %param.9) | copy-start | bytes 1179652
  0.0 19.9 %copy-start.2 = (bf16[256,768]{1,0:T(8,128)(2,1)S(1)}, bf16[256,768]{1,0:T(8,128)(2,1)}, u32[]{:S(2)}) copy-start(bf16[256,768]{1,0:T(8,128)(2,1)} %param.8) | copy-start | bytes 1179652
  1.0 1.5 %collective-permute-start = (bf16[1,32,1024]{2,1,0:T(8,128)(2,1)S(1)}, bf16[1,32,1024]{2,1,0:T(8,128)(2,1)S(1)}, u32[]{:S(2)}, u32[]{:S(2)}) collective-permute-start(bf16[1,32,1024]{2,1,0:T(8,128)(2,1)S(1)} %fusion.10), channel_id=1, source_target_pairs={{0,1},{1,0},{2,3},{3,2},{4,5},{5,4},{6,7},{7,6},{8,9},{9,8},{10,11... | collective-permute-start | bytes 196616 | tf_op jit(solution)/shard_map/ppermute | solution.py:24
  2.5 6.7 %collective-permute-start.1 = (bf16[2,32,1024]{2,1,0:T(8,128)(2,1)S(1)}, bf16[2,32,1024]{2,1,0:T(8,128)(2,1)S(1)}, u32[]{:S(2)}, u32[]{:S(2)}) collective-permute-start(bf16[2,32,1024]{2,1,0:T(8,128)(2,1)S(1)} %pad_maximum_fusion.3), channel_id=1, source_target_pairs={{0,2},{1,3},{2,0},{3,1},{4,6},{5,7},{6,4},{7,5},{8,10},{9,11},{10,... | collective-permute-start | bytes 393224 | tf_op jit(solution)/shard_map/ppermute | solution.py:24
  9.3 7.9 %collective-permute-start.2 = (bf16[4,32,1024]{2,1,0:T(8,128)(2,1)S(1)}, bf16[4,32,1024]{2,1,0:T(8,128)(2,1)S(1)}, u32[]{:S(2)}, u32[]{:S(2)}) collective-permute-start(bf16[4,32,1024]{2,1,0:T(8,128)(2,1)S(1)} %pad_maximum_fusion.2), channel_id=1, source_target_pairs={{0,4},{1,5},{2,6},{3,7},{4,0},{5,1},{6,2},{7,3},{8,12},{9,13},{10,... | collective-permute-start | bytes 786440 | tf_op jit(solution)/shard_map/ppermute | solution.py:24
  17.3 24.8 %collective-permute-start.3 = (bf16[8,32,1024]{2,1,0:T(8,128)(2,1)S(1)}, bf16[8,32,1024]{2,1,0:T(8,128)(2,1)S(1)}, u32[]{:S(2)}, u32[]{:S(2)}) collective-permute-start(bf16[8,32,1024]{2,1,0:T(8,128)(2,1)S(1)} %pad_maximum_fusion.1), channel_id=1, source_target_pairs={{0,8},{1,9},{2,10},{3,11},{4,12},{5,13},{6,14},{7,15},{8,0},{9,1},... | collective-permute-start | bytes 1572872 | tf_op jit(solution)/shard_map/ppermute | solution.py:24
  19.9 22.3 %copy-start = (f32[1024,768]{1,0:T(8,128)S(1)}, f32[1024,768]{1,0:T(8,128)}, u32[]{:S(2)}) copy-start(f32[1024,768]{1,0:T(8,128)} %param.5) | copy-start | bytes 9437188
